TPU v7x, 32 devices: a whole 2x2x4 slice. The times are simulated.
32 devices in a mesh: rows: 16 (over z, y, x), cols: 2 (over core).
Axes of the slice: x: 2, y: 2, z: 4, core: 2. Of those that a mesh axis runs over, the one named last changes fastest.
Arguments:
- parent_front: float32 [4096, 2048], P('rows', 'cols')
- right_sides: float32 [4096, 64], P('rows'), may hold values from -6 to 6
- child_values: float32 [1024, 1024], P('rows', 'cols'), may hold values from -6 to 6
- block_owner: int32 [256], P('rows'), may hold values from 0 to 15, as said below
- row_map: int32 [1024], P('rows'), may hold values from 0 to 255
- col_map: int32 [1024], P('cols'), may hold values from 0 to 1023, as said below
Outputs:
- updated: float32 [4096, 2048], P('rows', 'cols')
- side_coeffs: float32 [128, 64], replicated
- side_left: float32 [4096, 64], P('rows')
Inputs may be any that keep to these rules, and one draw needn't show every extreme that they name: `block_owner`: for every k, entries k * 16 to (k + 1) * 16 - 1 form a permutation of 0 to 15. `col_map`: each aligned run of 512 entries is strictly increasing, starts with 0 and ends with 1023.
All inputs are finite; a program needn't handle non-finite values.
Results may differ from a plain program's by a relative error of at most 0.0003.
Values sent between devices are 32-bit elements; how exact they have to be, the bound alone decides.
A program may use at most 64 MiB of HBM per device.

v0:
```python
import jax
import jax.numpy as jnp
from jax import lax
from jax.sharding import PartitionSpec as P

PANEL = 128
highest = lax.Precision.HIGHEST


def spread_2(value, axis, source):
    kept = jnp.where(lax.axis_index(axis) == source, value, 0).astype(value.dtype)
    return lax.psum(kept, axis)


def swapped(block, axis, stride):
    count = lax.axis_size(axis)
    route = []
    for low in range(count):
        high = low | 1 << stride
        if high != low and high < count:
            route += [(low, high), (high, low)]
    return lax.ppermute(block, axis, route)


def matmul(left, right):
    return jnp.dot(left, right, precision=highest, preferred_element_type=jnp.float32)


def lower_inverse(lower):
    order = lower.shape[0]
    if order <= 16:
        return jax.scipy.linalg.solve_triangular(
            lower, jnp.eye(order, dtype=jnp.float32), lower=True
        )
    half = order // 2
    first_inv = lower_inverse(lower[:half, :half])
    second_inv = lower_inverse(lower[half:, half:])
    corner = -matmul(second_inv, matmul(lower[half:, :half], first_inv))
    top = jnp.concatenate([first_inv, jnp.zeros((half, order - half), jnp.float32)], axis=1)
    bottom = jnp.concatenate([corner, second_inv], axis=1)
    return jnp.concatenate([top, bottom], axis=0)


def shards(parent_front, right_sides, child_values, block_owner, row_map, col_map):
    blocks_count = lax.axis_size("rows")
    rows_dev, cols_dev = parent_front.shape
    child_rows, child_cols = child_values.shape
    block_rows = child_rows // blocks_count
    grouped = child_values.reshape(blocks_count, block_rows, child_cols)
    targets = row_map.astype(jnp.float32).reshape(blocks_count, block_rows)
    ordered = jnp.zeros_like(grouped).at[block_owner].set(grouped)
    placed = jnp.zeros_like(targets).at[block_owner].set(targets)
    spread = (
        jnp.zeros((blocks_count, block_rows, cols_dev), jnp.float32).at[:, :, col_map].set(ordered)
    )
    arrived, landing = (
        lax.all_to_all(spread, "rows", split_axis=0, concat_axis=0, tiled=True),
        lax.all_to_all(placed, "rows", split_axis=0, concat_axis=0, tiled=True),
    )
    where_rows = landing.reshape(-1).astype(jnp.int32)
    assembled = parent_front.at[where_rows].add(arrived.reshape(-1, cols_dev))
    panel_rows = spread_2(assembled[:, :PANEL], "cols", 0)
    stacked = jnp.concatenate([assembled, right_sides], axis=1)
    products = matmul(panel_rows.T, stacked)
    gram_matrix = matmul(panel_rows.T, panel_rows)
    lower = jnp.linalg.cholesky(gram_matrix)
    inverse = lower_inverse(lower)
    reduced = matmul(inverse, products)
    upper = lower.T
    levels = blocks_count.bit_length() - 1
    for level in range(levels):
        packed = jnp.concatenate([upper, reduced], axis=1)
        partner = swapped(packed, "rows", level)
        other_upper = partner[:, :PANEL]
        other_reduced = partner[:, PANEL:]
        node_gram = matmul(upper.T, upper) + matmul(other_upper.T, other_upper)
        lower = jnp.linalg.cholesky(node_gram)
        inverse = lower_inverse(lower)
        joined = matmul(upper.T, reduced) + matmul(other_upper.T, other_reduced)
        reduced = matmul(inverse, joined)
        upper = lower.T
    coefs = matmul(inverse.T, reduced)
    remainder = stacked - matmul(panel_rows, coefs)
    updated = remainder[:, :cols_dev]
    side_left = remainder[:, cols_dev:]
    side_coeffs = coefs[:, cols_dev:]
    return (updated, side_coeffs, side_left)


def solution(mesh):
    in_specs = (
        P("rows", "cols"),
        P("rows", None),
        P("rows", "cols"),
        P("rows"),
        P("rows"),
        P("cols"),
    )
    out_specs = (P("rows", "cols"), P(), P("rows", None))
    return jax.shard_map(shards, mesh=mesh, in_specs=in_specs, out_specs=out_specs, check_vma=False)
```

profile of v0, /device:TPU:0, one launch (start us, length us, event | category | flops | bytes accessed | tf_op | source)
XLA Modules:
  0.0 306.1 jit_solution(11291508165823120388)
XLA Ops:
  8.0 1.2 scatter_custom_fusion
  9.2 8.3 %all-to-all-start = ((f32[16,1,4]{2,1,0:T(1,128)}), f32[16,1,4]{2,1,0:T(1,128)S(1)}, u32[]{:S(2)}, u32[]{:S(2)}) async-start(f32[16,1,4]{2,1,0:T(1,128)} %bitcast.92), calls=%async_computation | async-start | bytes 16384 | tf_op jit(solution)/shard_map/all_to_all | solution.py:58
  19.3 13.6 %scatter_fusion.1 = f32[16,4,1024]{0,1,2:T(4,128)S(1)} fusion(f32[16,4,1024]{0,1,2:T(4,128)S(1)} %broadcast_in_dim.24, s32[512]{0:T(512)S(1)} %compare_select_fusion, f32[512,16,4]{1,2,0:T(4,128)S(1)} %copy.47), kind=kCustom, calls=%fused_computation.2 | custom fusion | bytes 395264 | tf_op jit(solution)/shard_map/scatter | solution.py:54
  32.9 1.4 copy.48
  34.3 7.0 %all-to-all-start.1 = ((f32[16,4,1024]{2,1,0:T(4,128)}), f32[16,4,1024]{2,1,0:T(4,128)S(1)}, u32[]{:S(2)}, u32[]{:S(2)}) async-start(f32[16,4,1024]{2,1,0:T(4,128)} %copy.48), calls=%async_computation.1 | async-start | bytes 524288 | tf_op jit(solution)/shard_map/all_to_all | solution.py:57
  41.6 9.1 %all-to-all-done.1 = f32[16,4,1024]{2,1,0:T(4,128)S(1)} async-done(((f32[16,4,1024]{2,1,0:T(4,128)}), f32[16,4,1024]{2,1,0:T(4,128)S(1)}, u32[]{:S(2)}, u32[]{:S(2)}) %all-to-all-start.1) | async-done | bytes 262176 | tf_op jit(solution)/shard_map/all_to_all | solution.py:57
  50.8 2.0 scatter_fusion.2
  53.9 15.6 %all-reduce.37.cloned.1.call-done = f32[256,128]{1,0:T(8,128)} async-done(((f32[256,128]{1,0:T(8,128)}), f32[256,128]{1,0:T(8,128)}) %all-reduce.37.cloned.1.call-update) | async-done | bytes 131088 | tf_op jit(solution)/shard_map/psum | solution.py:12
  69.5 1.4 fusion.448
  71.1 11.7 %cholesky.89 = f32[128,128]{1,0:T(8,128)S(1)} custom-call(f32[128,128]{1,0:T(8,128)S(1)} %fusion.141), custom_call_target="Cholesky" | custom-call | tf_op jit(solution)/shard_map/jit(cholesky)/cholesky | solution.py:66
  84.2 1.2 custom-call.46
  85.9 1.2 custom-call.50
  87.6 1.2 custom-call.48
  89.2 1.2 custom-call.49
  91.8 1.2 custom-call.44
  93.3 1.2 custom-call.45
  95.2 1.2 custom-call.47
  97.2 1.2 custom-call.51
  99.3 1.0 fusion
  101.1 1.8 collective-permute-start
  103.8 13.6 %collective-permute-done = f32[128,1216]{0,1:T(8,128)S(1)} collective-permute-done((f32[128,1216]{0,1:T(8,128)S(1)}, f32[128,1216]{0,1:T(8,128)S(1)}, u32[]{:S(2)}, u32[]{:S(2)}) %collective-permute-start) | collective-permute-done | bytes 622624 | tf_op jit(solution)/shard_map/ppermute | solution.py:22
  117.7 11.8 %cholesky.100 = f32[128,128]{1,0:T(8,128)S(1)} custom-call(f32[128,128]{1,0:T(8,128)S(1)} %fusion.140), custom_call_target="Cholesky" | custom-call | tf_op jit(solution)/shard_map/jit(cholesky)/cholesky | solution.py:77
  131.7 1.2 custom-call.54
  133.3 1.2 custom-call.58
  135.0 1.2 custom-call.56
  136.6 1.2 custom-call.57
  138.5 1.2 custom-call.52
  140.1 1.2 custom-call.53
  141.9 1.2 custom-call.55
  144.0 1.2 custom-call.59
  147.4 1.8 collective-permute-start.1
  150.1 12.7 %collective-permute-done.1 = f32[128,1216]{0,1:T(8,128)S(1)} collective-permute-done((f32[128,1216]{0,1:T(8,128)S(1)}, f32[128,1216]{0,1:T(8,128)S(1)}, u32[]{:S(2)}, u32[]{:S(2)}) %collective-permute-start.1) | collective-permute-done | bytes 622624 | tf_op jit(solution)/shard_map/ppermute | solution.py:22
  163.2 11.7 %cholesky.111 = f32[128,128]{1,0:T(8,128)S(1)} custom-call(f32[128,128]{1,0:T(8,128)S(1)} %fusion.139), custom_call_target="Cholesky" | custom-call | tf_op jit(solution)/shard_map/jit(cholesky)/cholesky | solution.py:77
  177.0 1.2 custom-call.62
  178.7 1.2 custom-call.66
  180.3 1.2 custom-call.64
  182.0 1.2 custom-call.65
  183.9 1.2 custom-call.60
  185.4 1.2 custom-call.61
  187.2 1.2 custom-call.63
  189.3 1.2 custom-call.67
  192.7 1.8 collective-permute-start.2
  195.4 11.9 %collective-permute-done.2 = f32[128,1216]{0,1:T(8,128)S(1)} collective-permute-done((f32[128,1216]{0,1:T(8,128)S(1)}, f32[128,1216]{0,1:T(8,128)S(1)}, u32[]{:S(2)}, u32[]{:S(2)}) %collective-permute-start.2) | collective-permute-done | bytes 622624 | tf_op jit(solution)/shard_map/ppermute | solution.py:22
  207.6 11.9 %cholesky.122 = f32[128,128]{1,0:T(8,128)S(1)} custom-call(f32[128,128]{1,0:T(8,128)S(1)} %fusion.138), custom_call_target="Cholesky" | custom-call | tf_op jit(solution)/shard_map/jit(cholesky)/cholesky | solution.py:77
  221.6 1.2 custom-call.70
  223.3 1.2 custom-call.74
  225.0 1.2 custom-call.72
  226.6 1.2 custom-call.73
  228.5 1.2 custom-call.68
  230.1 1.2 custom-call.69
  231.9 1.2 custom-call.71
  234.0 1.2 custom-call.75
  237.3 2.7 collective-permute-start.3
  240.9 24.4 %collective-permute-done.3 = f32[128,1216]{0,1:T(8,128)S(1)} collective-permute-done((f32[128,1216]{0,1:T(8,128)S(1)}, f32[128,1216]{0,1:T(8,128)S(1)}, u32[]{:S(2)}, u32[]{:S(2)}) %collective-permute-start.3) | collective-permute-done | bytes 622624 | tf_op jit(solution)/shard_map/ppermute | solution.py:22
  265.7 11.7 %cholesky.133 = f32[128,128]{1,0:T(8,128)S(1)} custom-call(f32[128,128]{1,0:T(8,128)S(1)} %fusion.137), custom_call_target="Cholesky" | custom-call | tf_op jit(solution)/shard_map/jit(cholesky)/cholesky | solution.py:77
  278.8 1.2 custom-call.78
  280.5 1.2 custom-call.82
  282.1 1.2 custom-call.80
  283.8 1.2 custom-call.81
  285.7 1.2 custom-call.76
  287.2 1.4 custom-call.77
  289.2 1.2 custom-call.79
  291.3 1.2 custom-call.83
  297.7 1.3 copy.63
  (236 shorter events, 49.8 us)
Async XLA Ops:
  7.2 10.4 %copy-start.3 = (f32[64,512]{1,0:T(8,128)S(1)}, f32[64,512]{1,0:T(8,128)}, u32[]{:S(2)}) copy-start(f32[64,512]{1,0:T(8,128)} %param.11) | copy-start | bytes 393220
  7.2 0.7 copy-start.5
  7.2 0.7 copy-start.6
  7.2 10.3 %copy-start.4 = (s32[512]{0:T(512)S(1)}, s32[512]{0:T(512)}, u32[]{:S(2)}) copy-start(s32[512]{0:T(512)} %param.14) | copy-start | bytes 6148
  9.2 25.2 %all-to-all-start = ((f32[16,1,4]{2,1,0:T(1,128)}), f32[16,1,4]{2,1,0:T(1,128)S(1)}, u32[]{:S(2)}, u32[]{:S(2)}) async-start(f32[16,1,4]{2,1,0:T(1,128)} %bitcast.92), calls=%async_computation | async-start | bytes 16384 | tf_op jit(solution)/shard_map/all_to_all | solution.py:58
  34.3 16.5 %copy-start = (f32[256,1024]{1,0:T(8,128)S(1)}, f32[256,1024]{1,0:T(8,128)}, u32[]{:S(2)}) copy-start(f32[256,1024]{1,0:T(8,128)} %param.9) | copy-start | bytes 3145732
  34.3 16.4 %all-to-all-start.1 = ((f32[16,4,1024]{2,1,0:T(4,128)}), f32[16,4,1024]{2,1,0:T(4,128)S(1)}, u32[]{:S(2)}, u32[]{:S(2)}) async-start(f32[16,4,1024]{2,1,0:T(4,128)} %copy.48), calls=%async_computation.1 | async-start | bytes 524288 | tf_op jit(solution)/shard_map/all_to_all | solution.py:57
  41.4 28.1 %all-reduce.37.cloned.1.call-start = ((), (), s32[]{:S(2)}) async-start(), calls=%async_computation.2 | async-start | bytes 262144 | tf_op jit(solution)/shard_map/psum | solution.py:12
  53.9 45.4 %copy-start.2 = (f32[256,64]{0,1:T(8,128)S(1)}, f32[256,64]{0,1:T(8,128)}, u32[]{:S(2)}) copy-start(f32[256,64]{0,1:T(8,128)} %param.10) | copy-start | bytes 196612
  69.5 29.7 %copy-start.1 = (f32[256,128]{1,0:T(8,128)S(1)}, f32[256,128]{1,0:T(8,128)}, u32[]{:S(2)}) copy-start(f32[256,128]{1,0:T(8,128)} %all-reduce.37.cloned.1.call-done) | copy-start | bytes 393220
  101.1 16.3 %collective-permute-start = (f32[128,1216]{0,1:T(8,128)S(1)}, f32[128,1216]{0,1:T(8,128)S(1)}, u32[]{:S(2)}, u32[]{:S(2)}) collective-permute-start(f32[128,1216]{0,1:T(8,128)S(1)} %pad_maximum_fusion.2), channel_id=1, source_target_pairs={{0,2},{2,0},{4,6},{6,4},{8,10},{10,8},{12,14},{14,12},{16,18},{18,... | collective-permute-start | bytes 1867784 | tf_op jit(solution)/shard_map/ppermute | solution.py:22
  147.4 15.4 %collective-permute-start.1 = (f32[128,1216]{0,1:T(8,128)S(1)}, f32[128,1216]{0,1:T(8,128)S(1)}, u32[]{:S(2)}, u32[]{:S(2)}) collective-permute-start(f32[128,1216]{0,1:T(8,128)S(1)} %pad_maximum_fusion.3), channel_id=1, source_target_pairs={{0,4},{4,0},{2,6},{6,2},{8,12},{12,8},{10,14},{14,10},{16,20},{20,... | collective-permute-start | bytes 1867784 | tf_op jit(solution)/shard_map/ppermute | solution.py:22
  192.7 14.6 %collective-permute-start.2 = (f32[128,1216]{0,1:T(8,128)S(1)}, f32[128,1216]{0,1:T(8,128)S(1)}, u32[]{:S(2)}, u32[]{:S(2)}) collective-permute-start(f32[128,1216]{0,1:T(8,128)S(1)} %pad_maximum_fusion.4), channel_id=1, source_target_pairs={{0,8},{8,0},{2,10},{10,2},{4,12},{12,4},{6,14},{14,6},{16,24},{24,... | collective-permute-start | bytes 1867784 | tf_op jit(solution)/shard_map/ppermute | solution.py:22
  237.3 27.9 %collective-permute-start.3 = (f32[128,1216]{0,1:T(8,128)S(1)}, f32[128,1216]{0,1:T(8,128)S(1)}, u32[]{:S(2)}, u32[]{:S(2)}) collective-permute-start(f32[128,1216]{0,1:T(8,128)S(1)} %pad_maximum_fusion.5), channel_id=1, source_target_pairs={{0,16},{16,0},{2,18},{18,2},{4,20},{20,4},{6,22},{22,6},{8,24},{24... | collective-permute-start | bytes 1867784 | tf_op jit(solution)/shard_map/ppermute | solution.py:22
Sparse Core Ops, SparseCore 0:
  53.7 15.8 all-reduce.36
where the time goes:
time: 309 us; the launch traced here: 306 us
  other arithmetic  122 us (39%)
  waiting for transfers between devices  87.3 us (28%)
  matrix products  35.3 us (11%)
  starting transfers between devices  23.6 us (8%)
  local copies, waits for them, and re-layouts  22.5 us (7%)
  between operations  15.2 us (5%)
    ppermute x4, waiting for transfers between devices, swapped(): return lax.ppermute(block, axis, route)  62.6 us
    another operation x12, other arithmetic, shards(): lower = jnp.linalg.cholesky(node_gram)  49.9 us
    another operation x45, other arithmetic, lower_inverse(): jax.scipy.linalg.solve_triangular(lower, jnp.eye(order, dtype=jnp.float32...  49.9 us
    dot_general x95, matrix products, matmul(): jnp.dot(left, right, precision=highest, preferred_element_type=jnp.float32)  27.1 us
    psum x1, waiting for transfers between devices, spread_2(): return lax.psum(kept, axis)  15.6 us
    scatter x2, local copies, waits for them, and re-layouts, shards(): jnp.zeros((blocks_count, block_rows, cols_dev), jnp.float32)  15 us
    another operation x3, other arithmetic, shards(): lower = jnp.linalg.cholesky(gram_matrix)  12.4 us
    all_to_all x1, waiting for transfers between devices, shards(): lax.all_to_all(spread, 'rows', split_axis=0, concat_axis=0, tiled=True)  9.12 us
  transfers between devices with their start and end apart: 7, of which 6 were waited for; matrix products, arithmetic and copies ran while one was open for 7% of the time, Pallas kernels for 0%

commit v1 on v0

--- a/solution.py
+++ b/solution.py
@@ -9,7 +9,7 @@
 
 def spread_2(value, axis, source):
     kept = jnp.where(lax.axis_index(axis) == source, value, 0).astype(value.dtype)
-    return lax.psum(kept, axis)
+    return lax.all_gather(kept, axis).sum(axis=0)
 
 
 def swapped(block, axis, stride):

time: 309 us -> 280 us (0.906)
  between operations: 15.2 us -> 1.8 us
  waiting for transfers between devices: 87.3 us -> 75.6 us
  starting transfers between devices: 23.6 us -> 19.1 us
    psum x1 -> x0, waiting for transfers between devices: 15.6 us -> none  [spread_2(): return lax.psum(kept, axis)]
    ppermute x4, starting transfers between devices: 8.14 us -> 3.71 us  [swapped(): return lax.ppermute(block, axis, route)]
    ppermute x4, waiting for transfers between devices: 62.6 us -> 66.4 us  [swapped(): return lax.ppermute(block, axis, route)]
  transfers between devices with their start and end apart: 7 -> 6, of which waited for: 6 -> 5; matrix products, arithmetic and copies ran while one was open for 7% -> 7% of each run, Pallas kernels for 0% -> 0%
where the time goes in v1:
time: 280 us; the launch traced here: 277 us
  other arithmetic  121 us (43%)
  waiting for transfers between devices  75.6 us (27%)
  matrix products  34.2 us (12%)
  local copies, waits for them, and re-layouts  22.5 us (8%)
  starting transfers between devices  19.1 us (7%)
    ppermute x4, waiting for transfers between devices, swapped(): return lax.ppermute(block, axis, route)  66.4 us
    another operation x45, other arithmetic, lower_inverse(): jax.scipy.linalg.solve_triangular(lower, jnp.eye(order, dtype=jnp.float32...  49.9 us
    another operation x12, other arithmetic, shards(): lower = jnp.linalg.cholesky(node_gram)  49.9 us
    dot_general x95, matrix products, matmul(): jnp.dot(left, right, precision=highest, preferred_element_type=jnp.float32)  26 us
    scatter x2, local copies, waits for them, and re-layouts, shards(): jnp.zeros((blocks_count, block_rows, cols_dev), jnp.float32)  15 us
    another operation x3, other arithmetic, shards(): lower = jnp.linalg.cholesky(gram_matrix)  12.4 us
    all_to_all x1, waiting for transfers between devices, shards(): lax.all_to_all(spread, 'rows', split_axis=0, concat_axis=0, tiled=True)  9.17 us
    all_to_all x1, starting transfers between devices, shards(): lax.all_to_all(placed, 'rows', split_axis=0, concat_axis=0, tiled=True)  8.34 us
  transfers between devices with their start and end apart: 6, of which 5 were waited for; matrix products, arithmetic and copies ran while one was open for 7% of the time, Pallas kernels for 0%

profile of v1, /device:TPU:0, one launch (start us, length us, event | category | flops | bytes accessed | tf_op | source)
XLA Modules:
  0.0 276.9 jit_solution(575269598754322110)
XLA Ops:
  1.4 1.2 scatter_custom_fusion
  2.6 8.3 %all-to-all-start = ((f32[16,1,4]{2,1,0:T(1,128)}), f32[16,1,4]{2,1,0:T(1,128)S(1)}, u32[]{:S(2)}, u32[]{:S(2)}) async-start(f32[16,1,4]{2,1,0:T(1,128)} %bitcast.93), calls=%async_computation | async-start | bytes 16384 | tf_op jit(solution)/shard_map/all_to_all | solution.py:58
  11.1 1.0 scatter_fusion
  12.8 13.6 %scatter_fusion.1 = f32[16,4,1024]{0,1,2:T(4,128)S(1)} fusion(f32[16,4,1024]{0,1,2:T(4,128)S(1)} %broadcast_in_dim.24, s32[512]{0:T(512)S(1)} %compare_select_fusion, f32[512,16,4]{1,2,0:T(4,128)S(1)} %copy.47), kind=kCustom, calls=%fused_computation.2 | custom fusion | bytes 395264 | tf_op jit(solution)/shard_map/scatter | solution.py:54
  26.4 1.4 copy.48
  27.8 7.0 %all-to-all-start.1 = ((f32[16,4,1024]{2,1,0:T(4,128)}), f32[16,4,1024]{2,1,0:T(4,128)S(1)}, u32[]{:S(2)}, u32[]{:S(2)}) async-start(f32[16,4,1024]{2,1,0:T(4,128)} %copy.48), calls=%async_computation.1 | async-start | bytes 524288 | tf_op jit(solution)/shard_map/all_to_all | solution.py:57
  35.0 9.2 %all-to-all-done.1 = f32[16,4,1024]{2,1,0:T(4,128)S(1)} async-done(((f32[16,4,1024]{2,1,0:T(4,128)}), f32[16,4,1024]{2,1,0:T(4,128)S(1)}, u32[]{:S(2)}, u32[]{:S(2)}) %all-to-all-start.1) | async-done | bytes 262176 | tf_op jit(solution)/shard_map/all_to_all | solution.py:57
  44.3 1.5 scatter_fusion.2
  45.8 2.5 all-gather
  48.9 11.7 %cholesky.89 = f32[128,128]{1,0:T(8,128)S(1)} custom-call(f32[128,128]{1,0:T(8,128)S(1)} %fusion.141), custom_call_target="Cholesky" | custom-call | tf_op jit(solution)/shard_map/jit(cholesky)/cholesky | solution.py:66
  62.0 1.2 custom-call.46
  63.7 1.2 custom-call.50
  65.3 1.2 custom-call.48
  67.0 1.2 custom-call.49
  69.9 1.2 custom-call.44
  71.5 1.2 custom-call.45
  73.3 1.2 custom-call.47
  75.3 1.2 custom-call.51
  76.9 1.0 fusion
  79.2 0.8 collective-permute-start
  80.9 14.4 %collective-permute-done = f32[128,1216]{0,1:T(8,128)S(1)} collective-permute-done((f32[128,1216]{0,1:T(8,128)S(1)}, f32[128,1216]{0,1:T(8,128)S(1)}, u32[]{:S(2)}, u32[]{:S(2)}) %collective-permute-start) | collective-permute-done | bytes 622624 | tf_op jit(solution)/shard_map/ppermute | solution.py:22
  95.7 11.9 %cholesky.100 = f32[128,128]{1,0:T(8,128)S(1)} custom-call(f32[128,128]{1,0:T(8,128)S(1)} %fusion.140), custom_call_target="Cholesky" | custom-call | tf_op jit(solution)/shard_map/jit(cholesky)/cholesky | solution.py:77
  109.6 1.2 custom-call.54
  111.3 1.2 custom-call.58
  113.0 1.2 custom-call.56
  114.6 1.2 custom-call.57
  116.5 1.2 custom-call.52
  118.1 1.2 custom-call.53
  119.9 1.2 custom-call.55
  122.0 1.2 custom-call.59
  125.3 1.0 collective-permute-start.1
  127.2 13.4 %collective-permute-done.1 = f32[128,1216]{0,1:T(8,128)S(1)} collective-permute-done((f32[128,1216]{0,1:T(8,128)S(1)}, f32[128,1216]{0,1:T(8,128)S(1)}, u32[]{:S(2)}, u32[]{:S(2)}) %collective-permute-start.1) | collective-permute-done | bytes 622624 | tf_op jit(solution)/shard_map/ppermute | solution.py:22
  141.0 11.7 %cholesky.111 = f32[128,128]{1,0:T(8,128)S(1)} custom-call(f32[128,128]{1,0:T(8,128)S(1)} %fusion.139), custom_call_target="Cholesky" | custom-call | tf_op jit(solution)/shard_map/jit(cholesky)/cholesky | solution.py:77
  154.8 1.2 custom-call.62
  156.5 1.2 custom-call.66
  158.1 1.2 custom-call.64
  159.8 1.2 custom-call.65
  161.7 1.2 custom-call.60
  163.2 1.2 custom-call.61
  165.1 1.2 custom-call.63
  167.1 1.2 custom-call.67
  170.5 1.2 collective-permute-start.2
  172.5 12.4 %collective-permute-done.2 = f32[128,1216]{0,1:T(8,128)S(1)} collective-permute-done((f32[128,1216]{0,1:T(8,128)S(1)}, f32[128,1216]{0,1:T(8,128)S(1)}, u32[]{:S(2)}, u32[]{:S(2)}) %collective-permute-start.2) | collective-permute-done | bytes 622624 | tf_op jit(solution)/shard_map/ppermute | solution.py:22
  185.3 11.9 %cholesky.122 = f32[128,128]{1,0:T(8,128)S(1)} custom-call(f32[128,128]{1,0:T(8,128)S(1)} %fusion.138), custom_call_target="Cholesky" | custom-call | tf_op jit(solution)/shard_map/jit(cholesky)/cholesky | solution.py:77
  199.3 1.2 custom-call.70
  201.0 1.2 custom-call.74
  202.6 1.2 custom-call.72
  204.3 1.2 custom-call.73
  206.2 1.2 custom-call.68
  207.8 1.2 custom-call.69
  209.6 1.2 custom-call.71
  211.6 1.2 custom-call.75
  216.6 26.2 %collective-permute-done.3 = f32[128,1216]{0,1:T(8,128)S(1)} collective-permute-done((f32[128,1216]{0,1:T(8,128)S(1)}, f32[128,1216]{0,1:T(8,128)S(1)}, u32[]{:S(2)}, u32[]{:S(2)}) %collective-permute-start.3) | collective-permute-done | bytes 622624 | tf_op jit(solution)/shard_map/ppermute | solution.py:22
  243.2 11.7 %cholesky.133 = f32[128,128]{1,0:T(8,128)S(1)} custom-call(f32[128,128]{1,0:T(8,128)S(1)} %fusion.137), custom_call_target="Cholesky" | custom-call | tf_op jit(solution)/shard_map/jit(cholesky)/cholesky | solution.py:77
  256.4 1.2 custom-call.78
  258.0 1.2 custom-call.82
  259.7 1.2 custom-call.80
  261.3 1.2 custom-call.81
  263.2 1.2 custom-call.76
  264.8 1.5 custom-call.77
  266.8 1.2 custom-call.79
  268.9 1.2 custom-call.83
  272.9 1.0 convolution_subtract_fusion
  275.3 1.3 copy.63
  (233 shorter events, 48.1 us)
Async XLA Ops:
  0.6 10.4 %copy-start.2 = (f32[64,512]{1,0:T(8,128)S(1)}, f32[64,512]{1,0:T(8,128)}, u32[]{:S(2)}) copy-start(f32[64,512]{1,0:T(8,128)} %param.11) | copy-start | bytes 393220
  0.6 0.7 copy-start.4
  0.7 0.7 copy-start.5
  0.7 10.3 %copy-start.3 = (s32[512]{0:T(512)S(1)}, s32[512]{0:T(512)}, u32[]{:S(2)}) copy-start(s32[512]{0:T(512)} %param.14) | copy-start | bytes 6148
  2.6 25.2 %all-to-all-start = ((f32[16,1,4]{2,1,0:T(1,128)}), f32[16,1,4]{2,1,0:T(1,128)S(1)}, u32[]{:S(2)}, u32[]{:S(2)}) async-start(f32[16,1,4]{2,1,0:T(1,128)} %bitcast.93), calls=%async_computation | async-start | bytes 16384 | tf_op jit(solution)/shard_map/all_to_all | solution.py:58
  27.8 16.5 %copy-start = (f32[256,1024]{1,0:T(8,128)S(1)}, f32[256,1024]{1,0:T(8,128)}, u32[]{:S(2)}) copy-start(f32[256,1024]{1,0:T(8,128)} %param.9) | copy-start | bytes 3145732
  27.8 16.4 %all-to-all-start.1 = ((f32[16,4,1024]{2,1,0:T(4,128)}), f32[16,4,1024]{2,1,0:T(4,128)S(1)}, u32[]{:S(2)}, u32[]{:S(2)}) async-start(f32[16,4,1024]{2,1,0:T(4,128)} %copy.48), calls=%async_computation.1 | async-start | bytes 524288 | tf_op jit(solution)/shard_map/all_to_all | solution.py:57
  68.9 8.1 %copy-start.1 = (f32[256,64]{0,1:T(8,128)S(1)}, f32[256,64]{0,1:T(8,128)}, u32[]{:S(2)}) copy-start(f32[256,64]{0,1:T(8,128)} %param.10) | copy-start | bytes 196612
  79.2 16.1 %collective-permute-start = (f32[128,1216]{0,1:T(8,128)S(1)}, f32[128,1216]{0,1:T(8,128)S(1)}, u32[]{:S(2)}, u32[]{:S(2)}) collective-permute-start(f32[128,1216]{0,1:T(8,128)S(1)} %pad_maximum_fusion.2), channel_id=1, source_target_pairs={{0,2},{2,0},{4,6},{6,4},{8,10},{10,8},{12,14},{14,12},{16,18},{18,... | collective-permute-start | bytes 1867784 | tf_op jit(solution)/shard_map/ppermute | solution.py:22
  125.3 15.3 %collective-permute-start.1 = (f32[128,1216]{0,1:T(8,128)S(1)}, f32[128,1216]{0,1:T(8,128)S(1)}, u32[]{:S(2)}, u32[]{:S(2)}) collective-permute-start(f32[128,1216]{0,1:T(8,128)S(1)} %pad_maximum_fusion.3), channel_id=1, source_target_pairs={{0,4},{4,0},{2,6},{6,2},{8,12},{12,8},{10,14},{14,10},{16,20},{20,... | collective-permute-start | bytes 1867784 | tf_op jit(solution)/shard_map/ppermute | solution.py:22
  170.5 14.4 %collective-permute-start.2 = (f32[128,1216]{0,1:T(8,128)S(1)}, f32[128,1216]{0,1:T(8,128)S(1)}, u32[]{:S(2)}, u32[]{:S(2)}) collective-permute-start(f32[128,1216]{0,1:T(8,128)S(1)} %pad_maximum_fusion.4), channel_id=1, source_target_pairs={{0,8},{8,0},{2,10},{10,2},{4,12},{12,4},{6,14},{14,6},{16,24},{24,... | collective-permute-start | bytes 1867784 | tf_op jit(solution)/shard_map/ppermute | solution.py:22
  215.0 27.8 %collective-permute-start.3 = (f32[128,1216]{0,1:T(8,128)S(1)}, f32[128,1216]{0,1:T(8,128)S(1)}, u32[]{:S(2)}, u32[]{:S(2)}) collective-permute-start(f32[128,1216]{0,1:T(8,128)S(1)} %pad_maximum_fusion.5), channel_id=1, source_target_pairs={{0,16},{16,0},{2,18},{18,2},{4,20},{20,4},{6,22},{22,6},{8,24},{24... | collective-permute-start | bytes 1867784 | tf_op jit(solution)/shard_map/ppermute | solution.py:22
